TPU v7x, 32 devices: a whole 2x2x4 slice. The times are simulated.
32 devices in a mesh: strip: 2 (over y), col: 4 (over z), row: 4 (over x, core).
Axes of the slice: x: 2, y: 2, z: 4, core: 2. Of those that a mesh axis runs over, the one named last changes fastest.
Arguments:
- left_features: bfloat16 [64, 2048, 128], P(('strip', 'row'), 'col'), parts along dimension 0, may hold values from -6 to 6
- right_features: bfloat16 [64, 2048, 128], P(('strip', 'row'), 'col'), parts along dimension 0, may hold values from -6 to 6
- conv_first: bfloat16 [3, 3, 256, 256], replicated, may hold values from -0.125 to 0.125
- conv_second: bfloat16 [3, 3, 256, 256], replicated, may hold values from -0.125 to 0.125
Outputs:
- cost_field: bfloat16 [64, 2048, 256], P(('strip', 'row'), 'col'), parts along dimension 0
There are 2 independent parts, one for each index of `strip`. A program takes and returns all parts, laid end to end along the dimension named above; an argument that names none is the same for every part. Nothing has to cross between parts.
All inputs are finite; a program needn't handle non-finite values.
Results may differ from a plain program's by a relative error of at most 0.0058.
Values may be sent and summed in bfloat16 or wider, within the bound.
A program may use at most 128 MiB of HBM per device.

v0:
```python
import functools

import jax
import jax.numpy as jnp
from jax import lax
from jax.experimental import pallas as pl
from jax.experimental.pallas import tpu as pltpu
from jax.sharding import PartitionSpec as P

MESH = pl.DeviceIdType.MESH
F32 = jnp.float32
BF16 = jnp.bfloat16
G = 16
TILE = 112
LANES = 128


def kernel(
    ncol, nrow, left, right, w1_hbm, w2_hbm, out,
    rext, lext, rrev, vol3, hid3, w1, w2, lsem, ssem, rsem,
):
    rows, width, chans = left.shape
    disp = w1_hbm.shape[0] // 9
    col = lax.axis_index("col")
    row = lax.axis_index("row")
    has_l, has_r = col > 0, col < ncol - 1
    has_u, has_d = row > 0, row < nrow - 1
    to_l, to_r = {"col": col - 1}, {"col": col + 1}
    to_u, to_d = {"row": row - 1}, {"row": row + 1}
    reach = disp + G
    tiles = vol_cols(width) // TILE
    span = rext.shape[1]
    window = TILE_WINDOW(disp)
    hcols = width + G

    own = [
        pltpu.make_async_copy(right, rext.at[2 : rows + 2, reach : reach + width], lsem.at[0]),
        pltpu.make_async_copy(left, lext.at[2 : rows + 2, G : G + width], lsem.at[1]),
        pltpu.make_async_copy(w1_hbm, w1, lsem.at[2]),
        pltpu.make_async_copy(w2_hbm, w2, lsem.at[3]),
    ]
    for copy in own:
        copy.start()

    edge = reach + width
    rext[:, edge + G :] = jnp.zeros((rows + 4, span - edge - G, chans), BF16)
    lext[:, 2 * G + width :] = jnp.zeros((rows + 4, lext.shape[1] - 2 * G - width, chans), BF16)

    def clear(ref, *at):
        ref[at] = jnp.zeros(ref.at[at].shape, BF16)

    @pl.when(jnp.logical_not(has_l))
    def _():
        clear(rext, slice(0, rows + 4), slice(0, reach))
        clear(lext, slice(0, rows + 4), slice(0, G))

    @pl.when(jnp.logical_not(has_r))
    def _():
        clear(rext, slice(0, rows + 4), slice(edge, edge + G))
        clear(lext, slice(0, rows + 4), slice(G + width, 2 * G + width))

    @pl.when(jnp.logical_not(has_u))
    def _():
        clear(rext, slice(0, 2), slice(0, edge + G))
        clear(lext, slice(0, 2), slice(0, 2 * G + width))

    @pl.when(jnp.logical_not(has_d))
    def _():
        clear(rext, slice(rows + 2, rows + 4), slice(0, edge + G))
        clear(lext, slice(rows + 2, rows + 4), slice(0, 2 * G + width))

    barrier = pltpu.get_barrier_semaphore()
    for has, to in ((has_l, to_l), (has_r, to_r), (has_u, to_u), (has_d, to_d)):
        @pl.when(has)
        def _():
            pl.semaphore_signal(barrier, inc=1, device_id=to, device_id_type=MESH)
    peers = sum(has.astype(jnp.int32) for has in (has_l, has_r, has_u, has_d))
    pl.semaphore_wait(barrier, peers)

    counter = [0]

    def remote(src, dst, to):
        at = counter[0]
        counter[0] += 1
        return pltpu.make_async_remote_copy(
            src_ref=src, dst_ref=dst, send_sem=ssem.at[at], recv_sem=rsem.at[at],
            device_id=to, device_id_type=MESH,
        )

    tail = width - reach
    far = reach + width
    chunks = [(0, 2), (rows - 2, rows)]
    middle = rows // 2
    chunks += [(2, middle), (middle, rows - 2)]
    small_r = [remote(left.at[:, width - G : width], lext.at[2 : rows + 2, 0:G], to_r)]
    parts = [
        remote(right.at[a:b, tail:width], rext.at[2 + a : 2 + b, 0:reach], to_r)
        for a, b in chunks
    ]
    small_l = [
        remote(left.at[:, 0:G], lext.at[2 : rows + 2, G + width : 2 * G + width], to_l),
        remote(right.at[:, 0:G], rext.at[2 : rows + 2, far : far + G], to_l),
    ]
    down = [
        remote(right.at[rows - 2 : rows], rext.at[0:2, reach:far], to_d),
        remote(left.at[rows - 2 : rows], lext.at[0:2, G : G + width], to_d),
    ]
    up = [
        remote(right.at[0:2], rext.at[rows + 2 : rows + 4, reach:far], to_u),
        remote(left.at[0:2], lext.at[rows + 2 : rows + 4, G : G + width], to_u),
    ]

    def edges(source, target, to):
        s, t = slice(source, source + 2), slice(target, target + 2)
        return [
            remote(rext.at[s, 0:reach], rext.at[t, 0:reach], to),
            remote(rext.at[s, far : far + G], rext.at[t, far : far + G], to),
            remote(lext.at[s, 0:G], lext.at[t, 0:G], to),
            remote(lext.at[s, G + width : 2 * G + width], lext.at[t, G + width : 2 * G + width], to),
        ]

    up_edges = edges(2, rows + 2, to_u)
    down_edges = edges(rows, 0, to_d)

    def start(has, copies):
        @pl.when(has)
        def _():
            for copy in copies:
                copy.start()

    def recv(has, copies):
        @pl.when(has)
        def _():
            for copy in copies:
                copy.wait_recv()

    def sent(has, copies):
        @pl.when(has)
        def _():
            for copy in copies:
                copy.wait_send()

    start(has_r, small_r + parts)
    start(has_l, small_l)
    start(has_d, down)
    start(has_u, up)

    scale = 1.0 / jnp.sqrt(F32(chans))
    cut = -(-reach // TILE)
    fresh = -(-(span - TILE * cut) // (2 * G)) * (2 * G)

    def flip(size):
        i = lax.broadcasted_iota(jnp.int32, (size, size), 0)
        j = lax.broadcasted_iota(jnp.int32, (size, size), 1)
        return jnp.where(i + j == size - 1, 1.0, 0.0).astype(BF16)

    def correlate(first, count, right_part):
        size = fresh // 2 if right_part else (span - fresh) // 2
        base = 0 if right_part else fresh

        @pl.loop(0, count // 2)
        def _(p):
            pair = [first + 2 * p, first + 2 * p + 1]
            turn = flip(size)
            for q in range(2):
                for r in pair:
                    high = span - base - q * size
                    piece = jnp.dot(turn, rext[r, high - size : high, :], preferred_element_type=F32)
                    rrev[r, base + q * size : base + (q + 1) * size, :] = piece.astype(BF16)
            for t in range(cut, tiles) if right_part else range(cut):
                at = span - window - TILE * t
                for r in pair:
                    scores = lax.dot_general(
                        lext[r, TILE * t : TILE * (t + 1), :],
                        rrev[r, at : at + window, :],
                        (((1,), (1,)), ((), ())),
                        preferred_element_type=F32,
                    )
                    turned = pltpu.roll(
                        scores, window - TILE_SHIFT(disp), 1, stride=1, stride_axis=0
                    )[:, :disp]
                    value = (turned * scale).astype(BF16)
                    for b in range(3):
                        vol3[r, TILE * t + 2 - b : TILE * (t + 1) + 2 - b, b * disp : (b + 1) * disp] = value

    bar = -(-(TILE * cut + 2) // G) * G

    def first_conv(first, count, right_part):
        low, high = (bar, G + hcols) if right_part else (G, bar)
        size = high - low

        @pl.loop(0, count // 2)
        def _(p):
            g = first + 2 * p
            x = jnp.concatenate(
                [vol3[pl.ds(g + a, 2), low:high, :].reshape(2 * size, 3 * disp) for a in range(3)], axis=1
            )
            acc = jnp.dot(x, w1[...], preferred_element_type=F32)
            j = lax.broadcasted_iota(jnp.int32, (size, 1), 0)
            at_col = col * width + j + (low - G - 1)
            inside_col = (at_col >= 0) & (at_col < ncol * width)
            for k in range(2):
                at_row = row * rows + g + k - 1
                inside = inside_col & (at_row >= 0) & (at_row < nrow * rows)
                value = jnp.maximum(acc[k * size : (k + 1) * size], 0.0)
                value = jnp.where(inside, value, 0.0).astype(BF16)
                for b in range(3):
                    hid3[g + k, low - b : high - b, b * disp : (b + 1) * disp] = value

    def second_conv(first, count, right_part):
        low, high = (bar, G + width) if right_part else (G, bar)
        size = high - low

        @pl.loop(0, count // 2)
        def _(p):
            h = first + 2 * p
            x = jnp.concatenate(
                [hid3[pl.ds(h + a, 2), low:high, :].reshape(2 * size, 3 * disp) for a in range(3)], axis=1
            )
            acc = jnp.dot(x, w2[...], preferred_element_type=F32)
            out[pl.ds(h, 2), low - G : high - G] = jnp.maximum(acc, 0.0).astype(BF16).reshape(2, size, disp)

    RIGHT, LEFT = True, False
    own[0].wait()
    own[1].wait()
    recv(has_r, small_l)
    correlate(2, rows, RIGHT)
    recv(has_l, small_r + [parts[0]])
    start(has_u, up_edges)
    own[2].wait()
    first_conv(2, rows - 2, RIGHT)
    own[3].wait()
    second_conv(2, rows - 4, RIGHT)
    correlate(2, 2, LEFT)
    recv(has_l, [parts[1]])
    start(has_d, down_edges)
    correlate(rows, 2, LEFT)
    recv(has_d, up + up_edges)
    correlate(rows + 2, 2, RIGHT)
    correlate(rows + 2, 2, LEFT)
    first_conv(rows, 2, RIGHT)
    first_conv(rows, 2, LEFT)
    second_conv(rows - 2, 2, RIGHT)
    recv(has_l, [parts[2]])
    correlate(4, middle - 2, LEFT)
    first_conv(2, middle - 2, LEFT)
    recv(has_u, down + down_edges)
    correlate(0, 2, RIGHT)
    correlate(0, 2, LEFT)
    first_conv(0, 2, RIGHT)
    first_conv(0, 2, LEFT)
    second_conv(0, 2, RIGHT)
    second_conv(0, middle - 2, LEFT)
    recv(has_l, [parts[3]])
    correlate(middle + 2, rows - 2 - middle, LEFT)
    first_conv(middle, rows - middle, LEFT)
    second_conv(middle - 2, rows + 2 - middle, LEFT)

    sent(has_r, small_r + parts)
    sent(has_l, small_l)
    sent(has_d, down + down_edges)
    sent(has_u, up + up_edges)


def TILE_SHIFT(disp):
    return TILE_WINDOW(disp) - disp - 1


def vol_cols(width):
    return -(-(width + 2 * G) // TILE) * TILE


def TILE_WINDOW(disp):
    return -(-(TILE + disp - 1) // LANES) * LANES


def local(ncol, nrow, left, right, w1, w2):
    rows, width, chans = left.shape
    disp = w1.shape[2]
    outs = w1.shape[3]
    w1 = w1.reshape(-1, outs)
    w2 = w2.reshape(-1, outs)
    span = vol_cols(width) - TILE + TILE_WINDOW(disp)
    hbm = pl.BlockSpec(memory_space=pl.ANY)
    copies = 19
    return pl.pallas_call(
        functools.partial(fixed, ncol, nrow),
        out_shape=pltpu.VMEM((rows, width, outs), BF16),
        in_specs=[hbm] * 4,
        out_specs=pl.BlockSpec(memory_space=pltpu.VMEM),
        scratch_shapes=[
            pltpu.VMEM((rows + 4, span, chans), BF16),
            pltpu.VMEM((rows + 4, vol_cols(width), chans), BF16),
            pltpu.VMEM((rows + 4, span, chans), BF16),
            pltpu.VMEM((rows + 4, vol_cols(width) + G, 3 * disp), BF16),
            pltpu.VMEM((rows + 2, width + 3 * G, 3 * outs), BF16),
            pltpu.VMEM(w1.shape, BF16),
            pltpu.VMEM(w2.shape, BF16),
            pltpu.SemaphoreType.DMA((4,)),
            pltpu.SemaphoreType.DMA((copies,)),
            pltpu.SemaphoreType.DMA((copies,)),
        ],
        compiler_params=pltpu.CompilerParams(
            collective_id=0, has_side_effects=True, vmem_limit_bytes=67_043_328 - 2 * rows * width * outs - 2**18
        ),
    )(left, right, w1, w2)


def fixed(ncol, nrow, *refs):
    kernel(ncol, nrow, *refs)


def solution(mesh):
    in_specs = (P(("strip", "row"), "col", None), P(("strip", "row"), "col", None), P(), P())
    out_specs = P(("strip", "row"), "col", None)
    return jax.shard_map(
        functools.partial(local, mesh.shape["col"], mesh.shape["row"]),
        mesh=mesh, in_specs=in_specs, out_specs=out_specs, check_vma=False,
    )
```

profile of v0, /device:TPU:0, one launch (start us, length us, event | category | flops | bytes accessed | tf_op | source)
XLA Modules:
  0.0 32.3 jit_solution(13837900916153224544)
XLA Ops:
  0.0 31.0 %shard_map.46 = bf16[8,512,256]{2,1,0:T(8,128)(2,1)S(1)} custom-call(bf16[8,512,128]{2,1,0:T(8,128)(2,1)} %refs_0_.1, bf16[8,512,128]{2,1,0:T(8,128)(2,1)} %refs_1_.1, bf16[2304,256]{1,0:T(8,128)(2,1)} %bitcast.2, bf16[2304,256]{1,0:T(8,128)(2,1)} %bitcast.3), custom_call_target="tpu_custom_call" | custom-call | tf_op jit(solution)/shard_map/pallas_call | solution.py:286
  31.0 1.3 %copy.6 = bf16[8,512,256]{2,1,0:T(8,128)(2,1)} copy(bf16[8,512,256]{2,1,0:T(8,128)(2,1)S(1)} %shard_map.46) | data formatting | bytes 4194304
where the time goes:
time: 32.5 us; the launch traced here: 32.3 us
  Pallas kernels  31 us (95%)
  local copies, waits for them, and re-layouts  1.32 us (4%)
    pallas_call x1, Pallas kernels, local(): pl.pallas_call(functools.partial(fixed, ncol, nrow), out_shape=pltpu.VMEM...  31 us
    unnamed x1, local copies, waits for them, and re-layouts  1.32 us

commit v1 on v0

v1 whole, which is shorter than its diff:
```python
import functools

import jax
import jax.numpy as jnp
from jax import lax
from jax.experimental import pallas as pl
from jax.experimental.pallas import tpu as pltpu
from jax.sharding import PartitionSpec as P

MESH = pl.DeviceIdType.MESH
F32 = jnp.float32
BF16 = jnp.bfloat16
E = 16
G = 32
LANES = 128


def kernel(
    ncol, nrow, left, right, w1_hbm, w2_hbm, out,
    rext, lext, rrev, vol3, hid3, vrim, hrim, w1, w2, lsem, ssem, rsem,
):
    rows, width, chans = left.shape
    disp = w2_hbm.shape[1]
    col = lax.axis_index("col")
    row = lax.axis_index("row")
    has_l, has_r = col > 0, col < ncol - 1
    has_u, has_d = row > 0, row < nrow - 1
    to_l, to_r = {"col": col - 1}, {"col": col + 1}
    to_u, to_d = {"row": row - 1}, {"row": row + 1}
    halo = disp + E
    window = disp + LANES

    barrier = pltpu.get_barrier_semaphore()
    for has, to in ((has_l, to_l), (has_r, to_r), (has_u, to_u), (has_d, to_d)):
        @pl.when(has)
        def _():
            pl.semaphore_signal(barrier, inc=1, device_id=to, device_id_type=MESH)

    own = [
        pltpu.make_async_copy(right, rext.at[:, halo : halo + width], lsem.at[0]),
        pltpu.make_async_copy(left, lext.at[:, E : E + width], lsem.at[1]),
        pltpu.make_async_copy(w1_hbm, w1, lsem.at[2]),
        pltpu.make_async_copy(w2_hbm, w2, lsem.at[3]),
    ]
    for copy in own:
        copy.start()

    def clear(ref, *at):
        ref[at] = jnp.zeros(ref.at[at].shape, BF16)

    every = slice(0, rows)

    @pl.when(jnp.logical_not(has_l))
    def _():
        clear(rext, every, slice(0, halo))
        clear(lext, every, slice(0, E))

    @pl.when(jnp.logical_not(has_r))
    def _():
        clear(rext, every, slice(halo + width, halo + width + E))
        clear(lext, every, slice(E + width, 2 * E + width))

    @pl.when(jnp.logical_not(has_u))
    def _():
        clear(vrim, 0)
        clear(hrim, 0)

    @pl.when(jnp.logical_not(has_d))
    def _():
        clear(vrim, 1)
        clear(hrim, 1)

    peers = sum(has.astype(jnp.int32) for has in (has_l, has_r, has_u, has_d))
    pl.semaphore_wait(barrier, peers)

    counter = [0]

    def remote(src, dst, to):
        at = counter[0]
        counter[0] += 1
        return pltpu.make_async_remote_copy(
            src_ref=src, dst_ref=dst, send_sem=ssem.at[at], recv_sem=rsem.at[at],
            device_id=to, device_id_type=MESH,
        )

    def start(has, copies):
        @pl.when(has)
        def _():
            for copy in copies:
                copy.start()

    def recv(has, copies):
        @pl.when(has)
        def _():
            for copy in copies:
                copy.wait_recv()

    def sent(has, copies):
        @pl.when(has)
        def _():
            for copy in copies:
                copy.wait_send()

    b0, b1, b2, b3, b4 = -E, disp // 4, disp // 2, disp, width + E
    vcols = [(b3, b4), (b2, b3), (b1, b2), (b0, b1)]
    hcols = [(b3 + E, b4), (b2 + E, b3 + E), (b1 + E, b2 + E), (b0, b1 + E)]
    ocols = [(b3 + 2 * E, width), (b2 + 2 * E, b3 + 2 * E), (b1 + 2 * E, b2 + 2 * E), (0, b1 + 2 * E)]
    SA, SB, SC, SD = range(4)

    def halo_part(first, last, r0, r1):
        return remote(
            right.at[r0:r1, width + first : width + last],
            rext.at[r0:r1, halo + first : halo + last], to_r,
        )

    edge_l = [
        remote(left.at[:, 0:E], lext.at[:, E + width : 2 * E + width], to_l),
        remote(right.at[:, 0:E], rext.at[:, halo + width : halo + width + E], to_l),
    ]
    near = [halo_part(b2 - disp, 0, 0, rows)]
    mid = [halo_part(b1 - disp, b2 - disp, 0, rows)]
    edge_r = [remote(left.at[:, width - E : width], lext.at[:, 0:E], to_r)]
    far = [halo_part(b0 - disp, b1 - disp, r, r + 2) for r in (0, rows - 2)]
    far_rest = [halo_part(b0 - disp, b1 - disp, 2, rows - 2)]

    def rim(ref3, ref, cols):
        l, h = cols[0] + G, cols[1] + G
        mid_lanes = slice(disp, 2 * disp)
        up = remote(ref3.at[1, l:h, mid_lanes], ref.at[1, l:h], to_u)
        down = remote(ref3.at[rows, l:h, mid_lanes], ref.at[0, l:h], to_d)
        return [up], [down]

    vrims = [rim(vol3, vrim, c) for c in vcols]
    hrims = [rim(hid3, hrim, c) for c in hcols]

    start(has_l, edge_l)
    start(has_r, near + mid + edge_r)
    start(has_r, far + far_rest)

    scale = 1.0 / jnp.sqrt(F32(chans))

    def store3(ref3, r, first, value):
        n = value.shape[0]
        for b in range(3):
            at = first + G + 1 - b
            ref3[r, at : at + n, b * disp : (b + 1) * disp] = value

    def correlate(r, first, count):
        at = width + E - first - count
        scores = lax.dot_general(
            lext[r, first + E : first + E + count, :],
            rrev[r, at : at + window, :],
            (((1,), (1,)), ((), ())),
            preferred_element_type=F32,
        )
        i = lax.broadcasted_iota(jnp.int32, (count, LANES), 0)
        j = lax.broadcasted_iota(jnp.int32, (count, LANES), 1)
        ahead = i + j >= count - 1
        blocks = [scores[:, k : k + LANES] for k in range(0, window, LANES)]
        turned = [
            pltpu.roll(jnp.where(ahead, p, q), LANES + 1 - count, 1, stride=1, stride_axis=0)
            for p, q in zip(blocks, blocks[1:])
        ]
        store3(vol3, r + 1, first, (jnp.concatenate(turned, axis=1) * scale).astype(BF16))

    def flip(r, first, count):
        i = lax.broadcasted_iota(jnp.int32, (count, count), 0)
        j = lax.broadcasted_iota(jnp.int32, (count, count), 1)
        turn = jnp.where(i + j == count - 1, 1.0, 0.0).astype(BF16)
        pair = jnp.concatenate([rext[r + k, halo + first : halo + first + count, :] for k in range(2)], axis=1)
        piece = jnp.dot(turn, pair, preferred_element_type=F32).astype(BF16)
        at = width + E - first - count
        for k in range(2):
            rrev[r + k, at : at + count, :] = piece[:, k * chans : (k + 1) * chans]

    def tiles(cols):
        units = (cols[1] - cols[0]) // E
        n = -(-units * E // LANES)
        ends = [cols[0] + E * (units * k // n) for k in range(n + 1)]
        return [(p, q - p) for p, q in zip(ends, ends[1:])]

    def correlate_all(seg, per):
        @pl.loop(0, rows // per)
        def _(p):
            for k in range(per):
                for first, count in tiles(vcols[seg]):
                    correlate(p * per + k, first, count)

    def correlate_rows(seg, rs):
        for r in rs:
            for first, count in tiles(vcols[seg]):
                correlate(r, first, count)

    def send_rims(rims, seg):
        start(has_u, rims[seg][0])
        start(has_d, rims[seg][1])

    def take_rims(rims, ref, ref3, cols, seg):
        recv(has_d, rims[seg][0])
        recv(has_u, rims[seg][1])
        l, h = cols[seg]
        store3(ref3, 0, l, ref[0, l + G : h + G, :])
        store3(ref3, rows + 1, l, ref[1, l + G : h + G, :])

    def gathered(ref3, groups, l, h):
        return jnp.concatenate(
            [
                jnp.concatenate(
                    [ref3[pl.ds(g + a, n), l + G : h + G, :].reshape(n * (h - l), 3 * disp) for g, n in groups], axis=0
                )
                for a in range(3)
            ],
            axis=1,
        )

    def conv1(seg, groups):
        l, h = hcols[seg]
        size = h - l
        acc = jnp.dot(gathered(vol3, groups, l, h), w1[...], preferred_element_type=F32)
        masked = l < 0 or h > width
        if masked:
            at = col * width + l + lax.broadcasted_iota(jnp.int32, (size, 1), 0)
            inside = (at >= 0) & (at < ncol * width)
        k = 0
        for g, n in groups:
            for r in range(n):
                value = jnp.maximum(acc[k * size : (k + 1) * size], 0.0)
                if masked:
                    value = jnp.where(inside, value, 0.0)
                store3(hid3, g + r + 1, l, value.astype(BF16))
                k += 1

    def conv2(seg, groups):
        l, h = ocols[seg]
        size = h - l
        acc = jnp.dot(gathered(hid3, groups, l, h), w2[...], preferred_element_type=F32)
        acc = jnp.maximum(acc, 0.0).astype(BF16)
        k = 0
        for g, n in groups:
            out[pl.ds(g, n), l:h, :] = acc[k * size : (k + n) * size].reshape(n, size, disp)
            k += n

    half = rows // 2
    steps = rows // 4

    def inner(i):
        return [(half - 2 - 2 * i, 2), (half + 2 * i, 2)]

    def by_parts(conv, seg, last):
        @pl.loop(0, steps)
        def _(i):
            @pl.when(i == steps - 1)
            def _():
                last()
            conv(seg, inner(i))

    def take_v(seg):
        take_rims(vrims, vrim, vol3, vcols, seg)

    def take_h(seg):
        take_rims(hrims, hrim, hid3, hcols, seg)

    whole = [(0, rows)]

    def flip_all(cols, rs):
        for r in rs:
            for first, count in tiles(cols):
                flip(r, first, count)

    pairs = range(0, rows, 2)
    own[0].wait()
    own[1].wait()
    recv(has_r, edge_l)

    @pl.loop(0, half)
    def _(p):
        flip_all((0, width + E), [2 * p])

    correlate_all(SA, 2)
    send_rims(vrims, SA)
    own[2].wait()
    by_parts(conv1, SA, lambda: take_v(SA))
    send_rims(hrims, SA)
    own[3].wait()
    by_parts(conv2, SA, lambda: take_h(SA))
    recv(has_l, near)
    flip_all((b2 - disp, 0), pairs)
    correlate_all(SB, 4)
    send_rims(vrims, SB)
    take_v(SB)
    conv1(SB, whole)
    send_rims(hrims, SB)
    recv(has_l, mid)
    flip_all((b1 - disp, b2 - disp), pairs)
    correlate_all(SC, 4)
    send_rims(vrims, SC)
    take_h(SB)
    conv2(SB, whole)
    take_v(SC)
    conv1(SC, whole)
    send_rims(hrims, SC)
    ends = [0, 1, rows - 2, rows - 1]
    recv(has_l, edge_r + far)
    flip_all((b0 - disp, b1 - disp), [0, rows - 2])
    correlate_rows(SD, ends)
    send_rims(vrims, SD)
    take_h(SC)
    conv2(SC, whole)
    take_v(SD)
    conv1(SD, [(0, 1), (rows - 1, 1)])
    send_rims(hrims, SD)
    recv(has_l, far_rest)
    flip_all((b0 - disp, b1 - disp), range(2, rows - 2, 2))
    correlate_rows(SD, range(2, rows - 2))
    conv1(SD, [(1, rows - 2)])
    take_h(SD)
    conv2(SD, whole)

    sent(has_l, edge_l)
    sent(has_r, near + mid + edge_r + far + far_rest)
    for rims in (vrims, hrims):
        for up, down in rims:
            sent(has_u, up)
            sent(has_d, down)


def local(ncol, nrow, left, right, w1, w2):
    rows, width, chans = left.shape
    disp = w1.shape[2]
    outs = w1.shape[3]
    w1 = w1.reshape(-1, outs)
    w2 = w2.reshape(-1, outs)
    span = width + disp + 2 * E + LANES
    wide = width + 2 * G
    hbm = pl.BlockSpec(memory_space=pl.ANY)
    copies = 24
    return pl.pallas_call(
        functools.partial(fixed, ncol, nrow),
        out_shape=pltpu.VMEM((rows, width, outs), BF16),
        in_specs=[hbm] * 4,
        out_specs=pl.BlockSpec(memory_space=pltpu.VMEM),
        scratch_shapes=[
            pltpu.VMEM((rows, width + disp + 2 * E, chans), BF16),
            pltpu.VMEM((rows, width + 2 * E, chans), BF16),
            pltpu.VMEM((rows, span, chans), BF16),
            pltpu.VMEM((rows + 2, wide, 3 * disp), BF16),
            pltpu.VMEM((rows + 2, wide, 3 * outs), BF16),
            pltpu.VMEM((2, wide, disp), BF16),
            pltpu.VMEM((2, wide, outs), BF16),
            pltpu.VMEM(w1.shape, BF16),
            pltpu.VMEM(w2.shape, BF16),
            pltpu.SemaphoreType.DMA((4,)),
            pltpu.SemaphoreType.DMA((copies,)),
            pltpu.SemaphoreType.DMA((copies,)),
        ],
        compiler_params=pltpu.CompilerParams(
            collective_id=0, has_side_effects=True, vmem_limit_bytes=67_043_328 - 2 * rows * width * outs - 2**18
        ),
    )(left, right, w1, w2)


def fixed(ncol, nrow, *refs):
    kernel(ncol, nrow, *refs)


def solution(mesh):
    in_specs = (P(("strip", "row"), "col", None), P(("strip", "row"), "col", None), P(), P())
    out_specs = P(("strip", "row"), "col", None)
    return jax.shard_map(
        functools.partial(local, mesh.shape["col"], mesh.shape["row"]),
        mesh=mesh, in_specs=in_specs, out_specs=out_specs, check_vma=False,
    )
```

time: 32.5 us -> 42.4 us (1.30)
  the two profiles are of different devices: /device:TPU:0 before, /device:TPU:1 now
where the time goes in v1:
time: 42.4 us; the launch traced here: 42.3 us
  Pallas kernels  40.9 us (96%)
  local copies, waits for them, and re-layouts  1.32 us (3%)
    pallas_call x1, Pallas kernels, local(): pl.pallas_call(functools.partial(fixed, ncol, nrow), out_shape=pltpu.VMEM...  40.9 us
    unnamed x1, local copies, waits for them, and re-layouts  1.32 us

profile of v1, /device:TPU:1, one launch (start us, length us, event | category | flops | bytes accessed | tf_op | source)
XLA Modules:
  0.0 42.3 jit_solution(17566768708188642984)
XLA Ops:
  0.0 40.9 %shard_map.46 = bf16[8,512,256]{2,1,0:T(8,128)(2,1)S(1)} custom-call(bf16[8,512,128]{2,1,0:T(8,128)(2,1)} %refs_0_.1, bf16[8,512,128]{2,1,0:T(8,128)(2,1)} %refs_1_.1, bf16[2304,256]{1,0:T(8,128)(2,1)} %bitcast.2, bf16[2304,256]{1,0:T(8,128)(2,1)} %bitcast.3), custom_call_target="tpu_custom_call" | custom-call | tf_op jit(solution)/shard_map/pallas_call | solution.py:337
  40.9 1.3 %copy.6 = bf16[8,512,256]{2,1,0:T(8,128)(2,1)} copy(bf16[8,512,256]{2,1,0:T(8,128)(2,1)S(1)} %shard_map.46) | data formatting | bytes 4194304

commit v2 on v1

v2 whole, which is shorter than its diff:
```python
import functools

import jax
import jax.numpy as jnp
from jax import lax
from jax.experimental import pallas as pl
from jax.experimental.pallas import tpu as pltpu
from jax.sharding import PartitionSpec as P

MESH = pl.DeviceIdType.MESH
F32 = jnp.float32
BF16 = jnp.bfloat16
E = 16
G = 32
LANES = 128


def kernel(
    ncol, nrow, left, right, w1_hbm, w2_hbm, out,
    rext, lext, rrev, vmid, vout, hmid, hout, w1, w2, lsem, ssem, rsem,
):
    rows, width, chans = left.shape
    disp = w2_hbm.shape[1]
    col = lax.axis_index("col")
    row = lax.axis_index("row")
    has_l, has_r = col > 0, col < ncol - 1
    has_u, has_d = row > 0, row < nrow - 1
    to_l, to_r = {"col": col - 1}, {"col": col + 1}
    to_u, to_d = {"row": row - 1}, {"row": row + 1}
    halo = disp + E
    window = disp + LANES

    barrier = pltpu.get_barrier_semaphore()
    for has, to in ((has_l, to_l), (has_r, to_r), (has_u, to_u), (has_d, to_d)):
        @pl.when(has)
        def _():
            pl.semaphore_signal(barrier, inc=1, device_id=to, device_id_type=MESH)

    own = [
        pltpu.make_async_copy(right, rext.at[:, halo : halo + width], lsem.at[0]),
        pltpu.make_async_copy(left, lext.at[:, E : E + width], lsem.at[1]),
        pltpu.make_async_copy(w1_hbm, w1, lsem.at[2]),
        pltpu.make_async_copy(w2_hbm, w2, lsem.at[3]),
    ]
    for copy in own:
        copy.start()

    def clear(ref, *at):
        ref[at] = jnp.zeros(ref.at[at].shape, BF16)

    every = slice(0, rows)

    @pl.when(jnp.logical_not(has_l))
    def _():
        clear(rext, every, slice(0, halo))
        clear(lext, every, slice(0, E))

    @pl.when(jnp.logical_not(has_r))
    def _():
        clear(rext, every, slice(halo + width, halo + width + E))
        clear(lext, every, slice(E + width, 2 * E + width))

    @pl.when(jnp.logical_not(has_u))
    def _():
        clear(vmid, slice(0, 2))

    @pl.when(jnp.logical_not(has_d))
    def _():
        clear(vmid, slice(rows + 2, rows + 4))

    peers = sum(has.astype(jnp.int32) for has in (has_l, has_r, has_u, has_d))

    counter = [0]

    def remote(src, dst, to):
        at = counter[0]
        counter[0] += 1
        return pltpu.make_async_remote_copy(
            src_ref=src, dst_ref=dst, send_sem=ssem.at[at], recv_sem=rsem.at[at],
            device_id=to, device_id_type=MESH,
        )

    def start(has, copies):
        @pl.when(has)
        def _():
            for copy in copies:
                copy.start()

    def recv(has, copies):
        @pl.when(has)
        def _():
            for copy in copies:
                copy.wait_recv()

    def sent(has, copies):
        @pl.when(has)
        def _():
            for copy in copies:
                copy.wait_send()

    b0, b1, b2, b3, b4 = -E, 5 * E, 11 * E, disp, width - E
    vcols = [[(b3, b4)], [(b2, b3), (b4, width + E)], [(b1, b2)], [(b0, b1)]]
    hcols = [[(b3 + E, b4 - E)], [(b2 + E, b3 + E), (b4 - E, width + E)], [(b1 + E, b2 + E)], [(b0, b1 + E)]]
    ocols = [
        [(b3 + 2 * E, b4 - 2 * E)],
        [(b2 + 2 * E, b3 + 2 * E), (b4 - 2 * E, width)],
        [(b1 + 2 * E, b2 + 2 * E)],
        [(0, b1 + 2 * E)],
    ]
    SA, SB, SC, SD = range(4)

    def halo_part(first, last, r0, r1):
        return remote(
            right.at[r0:r1, width + first : width + last],
            rext.at[r0:r1, halo + first : halo + last], to_r,
        )

    edge_l = [
        remote(left.at[:, 0:E], lext.at[:, E + width : 2 * E + width], to_l),
        remote(right.at[:, 0:E], rext.at[:, halo + width : halo + width + E], to_l),
    ]
    near = [halo_part(b2 - disp, 0, 0, rows)]
    mid = [halo_part(b1 - disp, b2 - disp, 0, rows)]
    edge_r = [remote(left.at[:, width - E : width], lext.at[:, 0:E], to_r)]
    far = [halo_part(b0 - disp, b1 - disp, r, r + 2) for r in (0, rows - 2)]
    far_rest = [halo_part(b0 - disp, b1 - disp, 2, rows - 2)]

    def rim(cols):
        ups, downs = [], []
        for c in cols:
            at = slice(c[0] + G, c[1] + G)
            ups.append(remote(vmid.at[2:4, at], vmid.at[rows + 2 : rows + 4, at], to_u))
            downs.append(remote(vmid.at[rows : rows + 2, at], vmid.at[0:2, at], to_d))
        return ups, downs

    rims = [rim(c) for c in vcols]

    once = (col >= 0).astype(jnp.int32)
    scale = 1.0 / jnp.sqrt(F32(chans))

    def spread(out_ref, r, first, value):
        n = value.shape[0]
        for b in (0, 1):
            at = first + G + 1 - 2 * b
            out_ref[r, at : at + n, b * disp : (b + 1) * disp] = value

    def store(mid_ref, out_ref, r, first, value):
        mid_ref[r, first + G : first + G + value.shape[0], :] = value
        spread(out_ref, r, first, value)

    def correlate(r, first, count):
        at = width + E - first - count
        scores = lax.dot_general(
            lext[r, first + E : first + E + count, :],
            rrev[r, at : at + window, :],
            (((1,), (1,)), ((), ())),
            preferred_element_type=F32,
        )
        i = lax.broadcasted_iota(jnp.int32, (count, LANES), 0)
        j = lax.broadcasted_iota(jnp.int32, (count, LANES), 1)
        ahead = i + j >= count - 1
        blocks = [scores[:, k : k + LANES] for k in range(0, window, LANES)]
        turned = [
            pltpu.roll(jnp.where(ahead, p, q), LANES + 1 - count, 1, stride=1, stride_axis=0)
            for p, q in zip(blocks, blocks[1:])
        ]
        store(vmid, vout, r + 2, first, (jnp.concatenate(turned, axis=1) * scale).astype(BF16))

    def flip(r, first, count):
        i = lax.broadcasted_iota(jnp.int32, (count, count), 0)
        j = lax.broadcasted_iota(jnp.int32, (count, count), 1)
        turn = jnp.where(i + j == count - 1, 1.0, 0.0).astype(BF16)
        pair = jnp.concatenate([rext[r + k, halo + first : halo + first + count, :] for k in range(2)], axis=1)
        piece = jnp.dot(turn, pair, preferred_element_type=F32).astype(BF16)
        at = width + E - first - count
        for k in range(2):
            rrev[r + k, at : at + count, :] = piece[:, k * chans : (k + 1) * chans]

    def tiles(cols):
        units = (cols[1] - cols[0]) // E
        n = -(-units * E // LANES)
        ends = [cols[0] + E * (units * k // n) for k in range(n + 1)]
        return [(p, q - p) for p, q in zip(ends, ends[1:])]

    def correlate_rows(seg, rs):
        for r in rs:
            for cols in vcols[seg]:
                for first, count in tiles(cols):
                    correlate(r, first, count)

    def correlate_loop(seg, first, n, per):
        @pl.loop(0, n // per)
        def _(p):
            correlate_rows(seg, [first + p * per + k for k in range(per)])

    def flip_rows(cols, rs):
        for r in rs:
            for first, count in tiles(cols):
                flip(r, first, count)

    def send_rims(seg):
        start(has_u, rims[seg][0])
        start(has_d, rims[seg][1])

    def take_rims(seg):
        recv(has_d, rims[seg][0])
        recv(has_u, rims[seg][1])
        for l, h in vcols[seg]:
            for r in (0, 1, rows + 2, rows + 3):
                spread(vout, r, l, vmid[r, l + G : h + G, :])

    def gathered(mid_ref, out_ref, shift, parts):
        taps = [(out_ref, slice(0, disp)), (mid_ref, slice(0, disp)), (out_ref, slice(disp, 2 * disp))]
        return jnp.concatenate(
            [
                jnp.concatenate(
                    [
                        ref[pl.ds(g + a + shift, n), l + G : h + G, lanes].reshape(n * (h - l), disp)
                        for g, n, (l, h) in parts
                    ],
                    axis=0,
                )
                for a in range(3)
                for ref, lanes in taps
            ],
            axis=1,
        )

    def apart(body):
        @pl.loop(0, once)
        def _(_):
            body()

    def shares(parts):
        total = sum(n * (h - l) for _, n, (l, h) in parts)
        first, second, done = [], [], 0
        for g, n, (l, h) in parts:
            take = min(n, max(0, round((total / 2 - done) / (h - l))))
            if take:
                first.append((g, take, (l, h)))
                done += take * (h - l)
            if take < n:
                second.append((g + take, n - take, (l, h)))
        return [p for p in (first, second) if p]

    def conv1(parts):
        @apart
        def _():
            for share in shares(parts):
                conv1_share(share)

    def conv2(parts):
        @apart
        def _():
            for share in shares(parts):
                conv2_share(share)

    def conv1_share(parts):
        acc = jnp.dot(gathered(vmid, vout, 1, parts), w1[...], preferred_element_type=F32)
        at = 0
        for g, n, (l, h) in parts:
            size = h - l
            masked = l < 0 or h > width
            if masked:
                x = col * width + l + lax.broadcasted_iota(jnp.int32, (size, 1), 0)
                inside = (x >= 0) & (x < ncol * width)
            for r in range(g, g + n):
                value = jnp.maximum(acc[at : at + size], 0.0)
                if masked:
                    value = jnp.where(inside, value, 0.0)
                if r < 0 or r >= rows:
                    value = jnp.where(has_u if r < 0 else has_d, value, 0.0)
                store(hmid, hout, r + 1, l, value.astype(BF16))
                at += size

    def conv2_share(parts):
        acc = jnp.dot(gathered(hmid, hout, 0, parts), w2[...], preferred_element_type=F32)
        acc = jnp.maximum(acc, 0.0).astype(BF16)
        at = 0
        for g, n, (l, h) in parts:
            size = n * (h - l)
            out[pl.ds(g, n), l:h, :] = acc[at : at + size].reshape(n, h - l, disp)
            at += size

    def parts_of(groups, cols):
        return [(g, n, c) for g, n in groups for c in cols]

    def hid_inner(seg):
        return parts_of([(1, rows - 2)], hcols[seg])

    def hid_outer(seg):
        return parts_of([(-1, 2), (rows - 1, 2)], hcols[seg])

    def out_inner(seg):
        return parts_of([(2, rows - 4)], ocols[seg])

    def out_outer(seg):
        return parts_of([(0, 2), (rows - 2, 2)], ocols[seg])

    outer_rows = [0, 1, rows - 2, rows - 1]
    pairs = range(0, rows, 2)
    pl.semaphore_wait(barrier, peers)
    start(has_l, edge_l)
    start(has_r, near + mid + edge_r + far + far_rest)
    own[0].wait()

    @pl.loop(0, rows // 2)
    def _(p):
        flip_rows((0, width), [2 * p])

    own[1].wait()

    @pl.loop(0, 2)
    def _(p):
        correlate_rows(SA, [(rows - 2) * p, (rows - 2) * p + 1])

    send_rims(SA)
    correlate_loop(SA, 2, rows - 4, 2)
    own[2].wait()
    conv1(hid_inner(SA))
    own[3].wait()
    conv2(out_inner(SA))

    recv(has_r, edge_l)
    recv(has_l, near)
    flip_rows((b2 - disp, 0), pairs)
    flip_rows((width, width + E), pairs)
    correlate_loop(SB, 0, rows, 4)
    send_rims(SB)
    take_rims(SA)
    conv1(hid_outer(SA) + hid_inner(SB))
    conv2(out_outer(SA) + out_inner(SB))

    recv(has_l, mid)
    flip_rows((b1 - disp, b2 - disp), pairs)
    correlate_loop(SC, 0, rows, 4)
    send_rims(SC)
    take_rims(SB)
    conv1(hid_outer(SB) + hid_inner(SC))
    conv2(out_outer(SB) + out_inner(SC))

    recv(has_l, edge_r + far)
    flip_rows((b0 - disp, b1 - disp), [0, rows - 2])
    correlate_rows(SD, outer_rows)
    send_rims(SD)
    recv(has_l, far_rest)
    flip_rows((b0 - disp, b1 - disp), range(2, rows - 2, 2))
    correlate_rows(SD, range(2, rows - 2))
    take_rims(SC)
    conv1(hid_outer(SC) + hid_inner(SD))
    conv2(out_outer(SC) + out_inner(SD))
    take_rims(SD)
    conv1(hid_outer(SD))
    conv2(out_outer(SD))

    sent(has_l, edge_l)
    sent(has_r, near + mid + edge_r + far + far_rest)
    for ups, downs in rims:
        sent(has_u, ups)
        sent(has_d, downs)


def local(ncol, nrow, left, right, w1, w2):
    rows, width, chans = left.shape
    disp = w1.shape[2]
    outs = w1.shape[3]
    w1 = w1.reshape(-1, outs)
    w2 = w2.reshape(-1, outs)
    span = width + disp + 2 * E + LANES
    wide = width + 2 * G
    hbm = pl.BlockSpec(memory_space=pl.ANY)
    copies = 18
    return pl.pallas_call(
        functools.partial(fixed, ncol, nrow),
        out_shape=pltpu.VMEM((rows, width, outs), BF16),
        in_specs=[hbm] * 4,
        out_specs=pl.BlockSpec(memory_space=pltpu.VMEM),
        scratch_shapes=[
            pltpu.VMEM((rows, width + disp + 2 * E, chans), BF16),
            pltpu.VMEM((rows, width + 2 * E, chans), BF16),
            pltpu.VMEM((rows, span, chans), BF16),
            pltpu.VMEM((rows + 4, wide, disp), BF16),
            pltpu.VMEM((rows + 4, wide, 2 * disp), BF16),
            pltpu.VMEM((rows + 2, wide, outs), BF16),
            pltpu.VMEM((rows + 2, wide, 2 * outs), BF16),
            pltpu.VMEM(w1.shape, BF16),
            pltpu.VMEM(w2.shape, BF16),
            pltpu.SemaphoreType.DMA((4,)),
            pltpu.SemaphoreType.DMA((copies,)),
            pltpu.SemaphoreType.DMA((copies,)),
        ],
        compiler_params=pltpu.CompilerParams(
            collective_id=0, has_side_effects=True, vmem_limit_bytes=67_043_328 - 2 * rows * width * outs - 2**18
        ),
    )(left, right, w1, w2)


def fixed(ncol, nrow, *refs):
    kernel(ncol, nrow, *refs)


def solution(mesh):
    in_specs = (P(("strip", "row"), "col", None), P(("strip", "row"), "col", None), P(), P())
    out_specs = P(("strip", "row"), "col", None)
    return jax.shard_map(
        functools.partial(local, mesh.shape["col"], mesh.shape["row"]),
        mesh=mesh, in_specs=in_specs, out_specs=out_specs, check_vma=False,
    )
```

time: 42.4 us -> 25 us (0.59)
  Pallas kernels: 40.9 us -> 23.5 us
    pallas_call x1, Pallas kernels: 40.9 us -> 23.5 us  [local(): pl.pallas_call(functools.partial(fixed, ncol, nrow), out_shape=pltpu.VMEM...]
where the time goes in v2:
time: 25 us; the launch traced here: 24.8 us
  Pallas kernels  23.5 us (94%)
  local copies, waits for them, and re-layouts  1.32 us (5%)
    pallas_call x1, Pallas kernels, local(): pl.pallas_call(functools.partial(fixed, ncol, nrow), out_shape=pltpu.VMEM...  23.5 us
    unnamed x1, local copies, waits for them, and re-layouts  1.32 us

profile of v2, /device:TPU:1, one launch (start us, length us, event | category | flops | bytes accessed | tf_op | source)
XLA Modules:
  0.0 24.8 jit_solution(5817576176903685316)
XLA Ops:
  0.0 23.5 %shard_map.46 = bf16[8,512,256]{2,1,0:T(8,128)(2,1)S(1)} custom-call(bf16[8,512,128]{2,1,0:T(8,128)(2,1)} %refs_0_.1, bf16[8,512,128]{2,1,0:T(8,128)(2,1)} %refs_1_.1, bf16[2304,256]{1,0:T(8,128)(2,1)} %bitcast.2, bf16[2304,256]{1,0:T(8,128)(2,1)} %bitcast.3), custom_call_target="tpu_custom_call" | custom-call | tf_op jit(solution)/shard_map/pallas_call | solution.py:373
  23.5 1.3 %copy.6 = bf16[8,512,256]{2,1,0:T(8,128)(2,1)} copy(bf16[8,512,256]{2,1,0:T(8,128)(2,1)S(1)} %shard_map.46) | data formatting | bytes 4194304

commit v3 on v2

--- a/solution.py
+++ b/solution.py
@@ -98,7 +98,7 @@
             for copy in copies:
                 copy.wait_send()
 
-    b0, b1, b2, b3, b4 = -E, 5 * E, 11 * E, disp, width - E
+    b0, b1, b2, b3, b4 = -E, 4 * E, 12 * E, disp, width - E
     vcols = [[(b3, b4)], [(b2, b3), (b4, width + E)], [(b1, b2)], [(b0, b1)]]
     hcols = [[(b3 + E, b4 - E)], [(b2 + E, b3 + E), (b4 - E, width + E)], [(b1 + E, b2 + E)], [(b0, b1 + E)]]
     ocols = [
@@ -188,11 +188,6 @@
                 for first, count in tiles(cols):
                     correlate(r, first, count)
 
-    def correlate_loop(seg, first, n, per):
-        @pl.loop(0, n // per)
-        def _(p):
-            correlate_rows(seg, [first + p * per + k for k in range(per)])
-
     def flip_rows(cols, rs):
         for r in rs:
             for first, count in tiles(cols):
@@ -299,23 +294,20 @@
 
     outer_rows = [0, 1, rows - 2, rows - 1]
     pairs = range(0, rows, 2)
+    own[0].wait()
+
+    flip_rows((0, width), pairs)
+
     pl.semaphore_wait(barrier, peers)
     start(has_l, edge_l)
     start(has_r, near + mid + edge_r + far + far_rest)
-    own[0].wait()
-
-    @pl.loop(0, rows // 2)
-    def _(p):
-        flip_rows((0, width), [2 * p])
 
     own[1].wait()
 
-    @pl.loop(0, 2)
-    def _(p):
-        correlate_rows(SA, [(rows - 2) * p, (rows - 2) * p + 1])
+    correlate_rows(SA, outer_rows)
 
     send_rims(SA)
-    correlate_loop(SA, 2, rows - 4, 2)
+    correlate_rows(SA, range(2, rows - 2))
     own[2].wait()
     conv1(hid_inner(SA))
     own[3].wait()
@@ -325,7 +317,7 @@
     recv(has_l, near)
     flip_rows((b2 - disp, 0), pairs)
     flip_rows((width, width + E), pairs)
-    correlate_loop(SB, 0, rows, 4)
+    correlate_rows(SB, range(rows))
     send_rims(SB)
     take_rims(SA)
     conv1(hid_outer(SA) + hid_inner(SB))
@@ -333,7 +325,7 @@
 
     recv(has_l, mid)
     flip_rows((b1 - disp, b2 - disp), pairs)
-    correlate_loop(SC, 0, rows, 4)
+    correlate_rows(SC, range(rows))
     send_rims(SC)
     take_rims(SB)
     conv1(hid_outer(SB) + hid_inner(SC))

time: 25 us -> 23.8 us (0.952)
  Pallas kernels: 23.5 us -> 22.3 us
    pallas_call x1, Pallas kernels: 23.5 us -> 22.3 us  [local(): pl.pallas_call(functools.partial(fixed, ncol, nrow), out_shape=pltpu.VMEM...]
where the time goes in v3:
time: 23.8 us; the launch traced here: 23.7 us
  Pallas kernels  22.3 us (94%)
  local copies, waits for them, and re-layouts  1.32 us (6%)
    pallas_call x1, Pallas kernels, local(): pl.pallas_call(functools.partial(fixed, ncol, nrow), out_shape=pltpu.VMEM...  22.3 us
    unnamed x1, local copies, waits for them, and re-layouts  1.32 us

profile of v3, /device:TPU:1, one launch (start us, length us, event | category | flops | bytes accessed | tf_op | source)
XLA Modules:
  0.0 23.7 jit_solution(1599037263595803974)
XLA Ops:
  0.0 22.3 %shard_map.46 = bf16[8,512,256]{2,1,0:T(8,128)(2,1)S(1)} custom-call(bf16[8,512,128]{2,1,0:T(8,128)(2,1)} %refs_0_.1, bf16[8,512,128]{2,1,0:T(8,128)(2,1)} %refs_1_.1, bf16[2304,256]{1,0:T(8,128)(2,1)} %bitcast.2, bf16[2304,256]{1,0:T(8,128)(2,1)} %bitcast.3), custom_call_target="tpu_custom_call" | custom-call | tf_op jit(solution)/shard_map/pallas_call | solution.py:365
  22.4 1.3 %copy.6 = bf16[8,512,256]{2,1,0:T(8,128)(2,1)} copy(bf16[8,512,256]{2,1,0:T(8,128)(2,1)S(1)} %shard_map.46) | data formatting | bytes 4194304

commit v4 on v3

--- a/solution.py
+++ b/solution.py
@@ -98,7 +98,7 @@
             for copy in copies:
                 copy.wait_send()
 
-    b0, b1, b2, b3, b4 = -E, 4 * E, 12 * E, disp, width - E
+    b0, b1, b2, b3, b4 = -E, 5 * E, 12 * E, disp, width - E
     vcols = [[(b3, b4)], [(b2, b3), (b4, width + E)], [(b1, b2)], [(b0, b1)]]
     hcols = [[(b3 + E, b4 - E)], [(b2 + E, b3 + E), (b4 - E, width + E)], [(b1 + E, b2 + E)], [(b0, b1 + E)]]
     ocols = [

time: 23.8 us -> 23.8 us (level)
  no operation moved by 1% of the time
where the time goes in v4:
time: 23.8 us; the launch traced here: 23.7 us
  Pallas kernels  22.4 us (94%)
  local copies, waits for them, and re-layouts  1.32 us (6%)
    pallas_call x1, Pallas kernels, local(): pl.pallas_call(functools.partial(fixed, ncol, nrow), out_shape=pltpu.VMEM...  22.4 us
    unnamed x1, local copies, waits for them, and re-layouts  1.32 us

profile of v4, /device:TPU:1, one launch (start us, length us, event | category | flops | bytes accessed | tf_op | source)
XLA Modules:
  0.0 23.7 jit_solution(882119138701703565)
XLA Ops:
  0.0 22.4 %shard_map.46 = bf16[8,512,256]{2,1,0:T(8,128)(2,1)S(1)} custom-call(bf16[8,512,128]{2,1,0:T(8,128)(2,1)} %refs_0_.1, bf16[8,512,128]{2,1,0:T(8,128)(2,1)} %refs_1_.1, bf16[2304,256]{1,0:T(8,128)(2,1)} %bitcast.2, bf16[2304,256]{1,0:T(8,128)(2,1)} %bitcast.3), custom_call_target="tpu_custom_call" | custom-call | tf_op jit(solution)/shard_map/pallas_call | solution.py:365
  22.4 1.3 %copy.6 = bf16[8,512,256]{2,1,0:T(8,128)(2,1)} copy(bf16[8,512,256]{2,1,0:T(8,128)(2,1)S(1)} %shard_map.46) | data formatting | bytes 4194304
